TPU v7x, 32 devices: a whole 2x2x4 slice. The times are simulated.
32 devices in a mesh: grp: 2 (over y), pool: 4 (over z), tp: 2 (over x), sub: 2 (over core).
Axes of the slice: x: 2, y: 2, z: 4, core: 2. Of those that a mesh axis runs over, the one named last changes fastest.
Arguments:
- queries: bfloat16 [128, 4096], P(('grp', 'pool', 'tp', 'sub')), parts along dimension 0, may hold values from -48 to 48
- keys_cache: bfloat16 [128, 512, 256], P(('grp', 'pool', 'tp', 'sub')), parts along dimension 0, may hold values from -6 to 6
- values_cache: bfloat16 [128, 512, 256], P(('grp', 'pool', 'tp', 'sub')), parts along dimension 0, may hold values from -6 to 6
- lengths: int32 [128], P(('grp', 'pool', 'tp', 'sub')), parts along dimension 0, may hold values from 2 to 512
- out_weight: bfloat16 [4096, 2048], P(('tp', 'sub')), may hold values from -0.75 to 0.75
- routes: int32 [128, 8], P(('grp', 'pool')), parts along dimension 0, may hold values from 0 to 63, all different within a row; in each aligned block of 16 rows (0 to 15, 16 to 31, ...) at most 14 rows name the same one
- route_weight: float32 [128, 8], P(('grp', 'pool')), parts along dimension 0, may hold values from 0.1 to 0.5
- expert_table: int32 [64], replicated, may hold values from 0 to 63, each once
- w_gate: bfloat16 [64, 768, 2048], P('pool', 'sub', 'tp'), may hold values from -0.125 to 0.125
- w_up: bfloat16 [64, 768, 2048], P('pool', 'sub', 'tp'), may hold values from -0.125 to 0.125
- w_down: bfloat16 [64, 768, 2048], P('pool', 'sub', 'tp'), may hold values from -0.875 to 0.875
Outputs:
- attended: bfloat16 [128, 2048], P(('grp', 'pool', 'tp', 'sub')), parts along dimension 0
- expert_out: bfloat16 [128, 2048], P(('grp', 'pool'), ('tp', 'sub')), parts along dimension 0
There are 2 independent parts, one for each index of `grp`. A program takes and returns all parts, laid end to end along the dimension named above; an argument that names none is the same for every part. Nothing has to cross between parts.
Inputs may be any that keep to these rules, and one draw needn't show every extreme that they name: `routes`: in each aligned block of 16 rows (the rows of one pool index) no expert is named by more than 14 rows, and in some block one expert is named by exactly 14 rows; each row names 8 different experts. `expert_table`: a permutation of the experts.
All inputs are finite; a program needn't handle non-finite values.
Results may differ from a plain program's by a relative error of at most 0.0086.
Values may be sent and summed in bfloat16 or wider, within the bound.
No kernel may reach another device: no remote copies, remote signals or barrier semaphores. Data moves between devices by JAX's collectives and lax.ppermute only.
A program may use at most 128 MiB of HBM per device.

v0:
```python
import math
import jax
import jax.numpy as jnp
from jax import lax
from jax.sharding import PartitionSpec as P

D = 2048
HEADS = 32
KV_HEADS = 2
HEAD_DIM = 128
EXPERTS = 64
TOP_K = 8
CAPACITY = 14
masked_low = -1e30


def body(
    queries,
    keys_cache,
    values_cache,
    lengths,
    out_weight,
    routes,
    route_weight,
    expert_table,
    w_gate,
    w_up,
    w_down,
):
    shard_index = lax.axis_index(("tp", "sub"))
    pool_count = lax.axis_size("pool")
    tp_count = lax.axis_size("tp")
    tp_index = lax.axis_index("tp")
    sub_count = lax.axis_size("sub")
    sub_index = lax.axis_index("sub")
    row_count = queries.shape[0]
    positions = keys_cache.shape[1]
    group_size = HEADS // KV_HEADS
    query_four = queries.reshape(row_count, KV_HEADS, group_size, HEAD_DIM)
    key_four = keys_cache.reshape(row_count, positions, KV_HEADS, HEAD_DIM)
    value_four = values_cache.reshape(row_count, positions, KV_HEADS, HEAD_DIM)
    scores = jnp.einsum(
        "rkgd,rlkd->rkgl", query_four, key_four, preferred_element_type=jnp.float32
    ) * (1.0 / math.sqrt(HEAD_DIM))
    in_range = (lax.iota(jnp.int32, positions)[None, :] < lengths[:, None])[:, None, None, :]
    masked = jnp.where(in_range, scores, masked_low)
    row_max = jnp.max(masked, axis=3, keepdims=True)
    exp_terms = jnp.where(in_range, jnp.exp(masked - row_max), 0.0)
    exp_sum = jnp.sum(exp_terms, axis=3)
    weights = exp_terms.astype(jnp.bfloat16)
    weighted = jnp.einsum(
        "rkgl,rlkd->rkgd", weights, value_four, preferred_element_type=jnp.float32
    )
    attention = (
        (weighted / exp_sum[..., None]).reshape(row_count, HEADS * HEAD_DIM).astype(jnp.bfloat16)
    )
    head_rows = lax.all_to_all(attention, ("tp", "sub"), split_axis=1, concat_axis=0, tiled=True)
    partial_value = jnp.dot(head_rows, out_weight, preferred_element_type=jnp.float32)
    summed = lax.psum(partial_value, ("tp", "sub"))
    attended_all = summed.astype(jnp.bfloat16)
    attended = lax.dynamic_slice_in_dim(attended_all, shard_index * row_count, row_count, 0)
    pool_rows = attended_all.shape[0]
    pair_count = pool_rows * TOP_K
    expert_ids = lax.iota(jnp.int32, EXPERTS)
    flat_routes = routes.reshape(pair_count)
    entry_index = jnp.sum(
        jnp.where(flat_routes[:, None] == expert_ids[None, :], expert_table[None, :], 0), axis=1
    )
    entry_hot = (entry_index[:, None] == expert_ids[None, :]).astype(jnp.int32)
    slot_rank = jnp.sum((jnp.cumsum(entry_hot, axis=0) - entry_hot) * entry_hot, axis=1)
    slot_index = entry_index * CAPACITY + slot_rank
    slot_total = EXPERTS * CAPACITY
    slot_hot = (slot_index[:, None] == lax.iota(jnp.int32, slot_total)[None, :]).astype(
        jnp.bfloat16
    )
    row_hot = (
        (lax.iota(jnp.int32, pair_count) // TOP_K)[:, None]
        == lax.iota(jnp.int32, pool_rows)[None, :]
    ).astype(jnp.bfloat16)
    placing = jnp.einsum("ps,pr->sr", slot_hot, row_hot, preferred_element_type=jnp.float32).astype(
        jnp.bfloat16
    )
    outgoing = jnp.dot(placing, attended_all, preferred_element_type=jnp.float32).astype(
        jnp.bfloat16
    )
    outgoing = outgoing.reshape(pool_count, EXPERTS // pool_count, CAPACITY, D)
    block_width = D // tp_count
    half_width = block_width // sub_count
    own_slice = lax.dynamic_slice_in_dim(
        outgoing, tp_index * block_width + sub_index * half_width, half_width, 3
    )
    arrived = lax.all_to_all(own_slice, "pool", split_axis=0, concat_axis=0, tiled=True)
    incoming = lax.all_gather(arrived, "sub", axis=3, tiled=True)
    gate_part = jnp.einsum("pjcd,jfd->pjcf", incoming, w_gate, preferred_element_type=jnp.float32)
    up_part = jnp.einsum("pjcd,jfd->pjcf", incoming, w_up, preferred_element_type=jnp.float32)
    gate_value, up_value = lax.psum((gate_part, up_part), "tp")
    hidden = (jax.nn.silu(gate_value) * up_value).astype(jnp.bfloat16)
    partial_rows = jnp.einsum("pjcf,jfd->pjcd", hidden, w_down, preferred_element_type=jnp.float32)
    expert_rows = lax.psum_scatter(partial_rows, "sub", scatter_dimension=3, tiled=True).astype(
        jnp.bfloat16
    )
    returned = lax.all_to_all(expert_rows, "pool", split_axis=0, concat_axis=0, tiled=True)
    flat_back = returned.reshape(slot_total, returned.shape[3])
    picked = jnp.take(flat_back, slot_index, axis=0).astype(jnp.float32)
    scaled = picked * route_weight.reshape(pair_count)[:, None]
    expert_out = jnp.sum(scaled.reshape(pool_rows, TOP_K, returned.shape[3]), axis=1).astype(
        jnp.bfloat16
    )
    return (attended, expert_out)


def solution(mesh):
    in_specs = (
        P(("grp", "pool", "tp", "sub"), None),
        P(("grp", "pool", "tp", "sub"), None, None),
        P(("grp", "pool", "tp", "sub"), None, None),
        P(("grp", "pool", "tp", "sub")),
        P(("tp", "sub"), None),
        P(("grp", "pool"), None),
        P(("grp", "pool"), None),
        P(),
        P("pool", "sub", "tp"),
        P("pool", "sub", "tp"),
        P("pool", "sub", "tp"),
    )
    out_specs = (P(("grp", "pool", "tp", "sub"), None), P(("grp", "pool"), ("tp", "sub")))
    return jax.shard_map(body, mesh=mesh, in_specs=in_specs, out_specs=out_specs, check_vma=False)
```

profile of v0, /device:TPU:0, one launch (start us, length us, event | category | flops | bytes accessed | tf_op | source)
XLA Modules:
  0.0 255.0 jit_solution(3014672523360081864)
XLA Ops:
  7.2 0.0 copy-start
  7.2 0.0 copy-start.3
  7.2 0.0 copy-start.5
  7.2 0.8 copy.48
  8.1 0.7 iota_compare_fusion.8
  8.8 0.0 copy-done
  8.8 0.4 fusion.16
  9.2 0.2 fusion.33
  9.4 1.5 fusion.17
  11.0 0.6 copy.36
  11.6 4.2 %all-to-all-start = ((bf16[4,4,1024]{2,0,1:T(4,128)(2,1)}), bf16[4,4,1024]{2,0,1:T(4,128)(2,1)S(1)}, u32[]{:S(2)}, u32[]{:S(2)}) async-start(bf16[4,4,1024]{2,0,1:T(4,128)(2,1)} %copy.36), calls=%async_computation | async-start | bytes 65536 | tf_op jit(solution)/shard_map/all_to_all | solution.py:57
  15.8 0.0 all-gather.2.cloned.1.call-start
  15.8 0.0 copy-done.3
  15.8 0.1 copy.37
  15.9 0.1 eq.26
  16.0 0.0 copy-done.5
  16.0 0.2 select_reduce_fusion.1
  16.1 0.1 fusion.26
  16.2 0.2 reduce_window_sum.11
  16.4 0.2 select_reduce_fusion
  16.6 3.1 %all-to-all-done = bf16[4,4,1024]{2,0,1:T(4,128)(2,1)S(1)} async-done(((bf16[4,4,1024]{2,0,1:T(4,128)(2,1)}), bf16[4,4,1024]{2,0,1:T(4,128)(2,1)S(1)}, u32[]{:S(2)}, u32[]{:S(2)}) %all-to-all-start) | async-done | bytes 32800 | tf_op jit(solution)/shard_map/all_to_all | solution.py:57
  19.7 2.8 %fusion.34 = f32[16,2048]{1,0:T(8,128)S(1)} fusion(bf16[16,1024]{1,0:T(8,128)(2,1)S(1)} %all_to_all.20, bf16[1024,2048]{1,0:T(8,128)(2,1)} %param.15), kind=kOutput, calls=%fused_computation.55 | convolution fusion | flops 67108864 | bytes 4358144 | tf_op jit(solution)/shard_map/dot_general | solution.py:58
  22.6 11.7 %all-reduce.5 = bf16[16,2048]{1,0:T(8,128)(2,1)S(1)} all-reduce(f32[16,2048]{1,0:T(8,128)S(1)} %fusion.34), channel_id=1, replica_groups=mesh['grp'=2,'pool'=4,'tp'=2,'sub'=2] {'tp','sub'}, use_global_device_ids=true, to_apply=%region_2.3 | all-reduce | flops 32768 | bytes 196608 | tf_op jit(solution)/shard_map/psum | solution.py:59
  34.3 3.2 %convolution_convert_fusion = bf16[896,2048]{1,0:T(8,128)(2,1)} fusion(bf16[16,2048]{1,0:T(8,128)(2,1)S(1)} %all-reduce.5, s32[128]{0:T(128)S(1)} %get-tuple-element.5, s32[128]{0:T(128)S(1)} %and_select_fusion), kind=kOutput, calls=%fused_computation.9 | convolution fusion | flops 64356352 | bytes 3736576 | tf_op jit(solution)/shard_map/dot_general | solution.py:83
  37.5 6.0 %reshape.116 = bf16[4,16,14,2048]{3,2,1,0:T(8,128)(2,1)} reshape(bf16[896,2048]{1,0:T(8,128)(2,1)} %convolution_convert_fusion) | data formatting | bytes 7340032 | tf_op jit(solution)/shard_map/reshape | solution.py:86
  43.5 1.3 constant_dynamic-slice_fusion
  44.8 0.5 copy.38
  45.4 28.3 %all_to_all.26 = bf16[4,16,14,512]{3,1,2,0:T(8,128)(2,1)S(1)} all-to-all(bf16[4,16,14,512]{3,1,2,0:T(8,128)(2,1)S(1)} %copy.38), channel_id=1, replica_groups=mesh['grp'=2,'pool'=4,'tp'=2,'sub'=2] {'pool'}, dimensions={0} | all-to-all | bytes 1835008 | tf_op jit(solution)/shard_map/all_to_all | solution.py:92
  73.7 1.5 copy.39
  75.2 0.0 all-gather.2.cloned.1.call-update
  75.2 0.0 all-reduce.4.cloned.1.call-start
  75.3 8.9 %all-gather.2.cloned.1.call-done = bf16[4,16,14,1024]{3,2,0,1:T(8,128)(2,1)} async-done(((bf16[4,16,14,512]{3,2,0,1:T(8,128)(2,1)}), bf16[4,16,14,1024]{3,2,0,1:T(8,128)(2,1)}) %all-gather.2.cloned.1.call-update) | async-done | bytes 1835024 | tf_op jit(solution)/shard_map/all_gather | solution.py:93
  84.1 0.0 copy-start.2
  84.1 10.5 %fusion.10 = f32[4,16,14,384]{3,2,0,1:T(8,128)} fusion(bf16[4,16,14,1024]{3,2,0,1:T(8,128)(2,1)} %all-gather.2.cloned.1.call-done, bf16[16,384,1024]{2,1,0:T(8,128)(2,1)} %param.20), kind=kOutput, calls=%fused_computation.12 | convolution fusion | flops 704643072 | bytes 15794176 | tf_op jit(solution)/shard_map/pjcd,jfd->pjcf/dot_general | solution.py:95
  94.6 0.0 copy-done.2
  94.6 9.8 %fusion.7 = f32[4,16,14,384]{3,2,0,1:T(8,128)} fusion(bf16[4,16,14,1024]{3,2,0,1:T(8,128)(2,1)S(1)} %copy-done.2, bf16[16,384,1024]{2,1,0:T(8,128)(2,1)} %param.19), kind=kOutput, calls=%fused_computation.11 | convolution fusion | flops 704643072 | bytes 15794176 | tf_op jit(solution)/shard_map/pjcd,jfd->pjcf/dot_general | solution.py:94
  104.4 0.0 all-reduce.4.cloned.1.call-update
  104.4 0.2 reduce-scatter.2.cloned.1.call-start
  104.7 87.0 %all-reduce.4.cloned.1.call-done = (f32[4,16,14,384]{3,2,0,1:T(8,128)}, f32[4,16,14,384]{3,2,0,1:T(8,128)}) async-done(((f32[4,16,14,384]{3,2,0,1:T(8,128)}, f32[4,16,14,384]{3,2,0,1:T(8,128)}), (f32[4,16,14,384]{3,2,0,1:T(8,128)}, f32[4,16,14,384]{3,2,0,1:T(8,128)})) %all-reduce.4.cloned.1.call-update) | async-done | bytes 2752528 | tf_op jit(solution)/shard_map/psum | solution.py:96
  191.7 7.9 %fusion.1 = f32[16,4,14,1024]{3,2,1,0:T(8,128)S(1)} fusion(bf16[16,384,1024]{2,1,0:T(8,128)(2,1)} %param.21, f32[4,16,14,384]{3,2,0,1:T(8,128)} %get-tuple-element.2, f32[4,16,14,384]{3,2,0,1:T(8,128)} %get-tuple-element.3), kind=kOutput, calls=%fused_computation.2 | convolution fusion | flops 706707456 | bytes 19005440 | tf_op jit(solution)/shard_map/pjcf,jfd->pjcd/dot_general | solution.py:98
  199.6 3.9 %copy.58 = f32[16,4,14,1024]{3,0,2,1:T(8,128)} copy(f32[16,4,14,1024]{3,2,1,0:T(8,128)S(1)} %fusion.1) | data formatting | bytes 7340032 | tf_op jit(solution)/shard_map/pjcf,jfd->pjcd/dot_general | solution.py:98
  203.5 0.0 reduce-scatter.2.cloned.1.call-update
  203.6 0.0 copy-start.4
  203.6 11.7 %reduce-scatter.2.cloned.1.call-done = f32[4,16,14,512]{3,1,2,0:T(8,128)} async-done(((f32[4,16,14,1024]{3,1,2,0:T(8,128)}), f32[4,16,14,512]{3,1,2,0:T(8,128)}) %reduce-scatter.2.cloned.1.call-update) | async-done | bytes 1835024 | tf_op jit(solution)/shard_map/reduce_scatter | solution.py:99
  215.3 2.6 %convert_element_type.45 = bf16[4,16,14,512]{3,1,2,0:T(8,128)(2,1)} convert(f32[4,16,14,512]{3,1,2,0:T(8,128)} %reduce-scatter.2.cloned.1.call-done) | non-fusion elementwise | flops 458752 | bytes 2752512 | tf_op jit(solution)/shard_map/convert_element_type | solution.py:99
  217.8 4.8 %all-to-all-start.2 = ((bf16[4,16,14,512]{3,1,2,0:T(8,128)(2,1)}), bf16[4,16,14,512]{3,1,2,0:T(8,128)(2,1)S(1)}, u32[]{:S(2)}, u32[]{:S(2)}) async-start(bf16[4,16,14,512]{3,1,2,0:T(8,128)(2,1)} %convert_element_type.45), calls=%async_computation.3 | async-start | bytes 1835008 | tf_op jit(solution)/shard_map/all_to_all | solution.py:102
  222.7 0.1 add.76
  222.7 0.0 copy-done.4
  222.7 0.1 copy.42
  222.8 0.6 constant_dynamic-slice_fusion.1
  223.5 22.6 %all-to-all-done.2 = bf16[4,16,14,512]{3,1,2,0:T(8,128)(2,1)S(1)} async-done(((bf16[4,16,14,512]{3,1,2,0:T(8,128)(2,1)}), bf16[4,16,14,512]{3,1,2,0:T(8,128)(2,1)S(1)}, u32[]{:S(2)}, u32[]{:S(2)}) %all-to-all-start.2) | async-done | bytes 917536 | tf_op jit(solution)/shard_map/all_to_all | solution.py:102
  246.1 0.0 copy-start.1
  246.1 0.5 copy.41
  246.6 0.3 reshape.117
  246.9 0.8 gather_fusion
  247.7 0.8 multiply_reduce_fusion
  248.5 0.0 copy-done.1
  (6 shorter events, 0.1 us)
Async XLA Ops:
  7.2 1.6 copy-start
  7.2 8.6 %copy-start.3 = (s32[16,8]{0,1:T(8,128)S(1)}, s32[16,8]{0,1:T(8,128)}, u32[]{:S(2)}) copy-start(s32[16,8]{0,1:T(8,128)} %param.16) | copy-start | bytes 1540
  7.2 8.8 %copy-start.5 = (s32[64]{0:T(128)S(1)}, s32[64]{0:T(128)}, u32[]{:S(2)}) copy-start(s32[64]{0:T(128)} %param.18) | copy-start | bytes 772
  11.6 8.2 %all-to-all-start = ((bf16[4,4,1024]{2,0,1:T(4,128)(2,1)}), bf16[4,4,1024]{2,0,1:T(4,128)(2,1)S(1)}, u32[]{:S(2)}, u32[]{:S(2)}) async-start(bf16[4,4,1024]{2,0,1:T(4,128)(2,1)} %copy.36), calls=%async_computation | async-start | bytes 65536 | tf_op jit(solution)/shard_map/all_to_all | solution.py:57
  15.8 68.3 %all-gather.2.cloned.1.call-start = ((), (), s32[]{:S(2)}) async-start(), calls=%async_computation.4 | async-start | bytes 3145728 | tf_op jit(solution)/shard_map/all_gather | solution.py:93
  75.2 116.5 %all-reduce.4.cloned.1.call-start = ((), (), s32[]{:S(2)}) async-start(), calls=%async_computation.6 | async-start | bytes 6291456 | tf_op jit(solution)/shard_map/psum | solution.py:96
  84.1 10.5 %copy-start.2 = (bf16[4,16,14,1024]{3,2,0,1:T(8,128)(2,1)S(1)}, bf16[4,16,14,1024]{3,2,0,1:T(8,128)(2,1)}, u32[]{:S(2)}) copy-start(bf16[4,16,14,1024]{3,2,0,1:T(8,128)(2,1)} %all-gather.2.cloned.1.call-done) | copy-start | bytes 5505028
  104.4 110.8 %reduce-scatter.2.cloned.1.call-start = ((), (), s32[]{:S(2)}) async-start(), calls=%async_computation.5 | async-start | bytes 5505024 | tf_op jit(solution)/shard_map/reduce_scatter | solution.py:99
  203.6 19.2 %copy-start.4 = (f32[16,8]{0,1:T(8,128)S(1)}, f32[16,8]{0,1:T(8,128)}, u32[]{:S(2)}) copy-start(f32[16,8]{0,1:T(8,128)} %param.17) | copy-start | bytes 1540
  217.8 28.2 %all-to-all-start.2 = ((bf16[4,16,14,512]{3,1,2,0:T(8,128)(2,1)}), bf16[4,16,14,512]{3,1,2,0:T(8,128)(2,1)S(1)}, u32[]{:S(2)}, u32[]{:S(2)}) async-start(bf16[4,16,14,512]{3,1,2,0:T(8,128)(2,1)} %convert_element_type.45), calls=%async_computation.3 | async-start | bytes 1835008 | tf_op jit(solution)/shard_map/all_to_all | solution.py:102
  246.1 2.4 copy-start.1
Sparse Core Ops, SparseCore 0:
  75.3 8.7 all-gather.1
  104.6 87.1 all-reduce.3
  203.7 11.5 reduce-scatter.1
where the time goes:
time: 256 us; the launch traced here: 255 us
  waiting for transfers between devices  133 us (52%)
  blocking collectives  40 us (16%)
  matrix products  36.2 us (14%)
  local copies, waits for them, and re-layouts  17.3 us (7%)
  between operations  13.9 us (5%)
  starting transfers between devices  9.29 us (4%)
  other arithmetic  4.91 us (2%)
    psum x1, waiting for transfers between devices, body(): gate_value, up_value = lax.psum((gate_part, up_part), 'tp')  87 us
    all_to_all x1, blocking collectives, body(): lax.all_to_all(own_slice, 'pool', split_axis=0, concat_axis=0, tiled=True)  28.3 us
    all_to_all x1, waiting for transfers between devices, body(): lax.all_to_all(expert_rows, 'pool', split_axis=0, concat_axis=0, tiled=True)  22.6 us
    psum x1, blocking collectives, body(): summed = lax.psum(partial_value, ('tp', 'sub'))  11.7 us
    reduce_scatter x1, waiting for transfers between devices, body(): lax.psum_scatter(partial_rows, 'sub', scatter_dimension=3, tiled=True)  11.7 us
    dot_general x1, matrix products, body(): jnp.einsum('pjcd,jfd->pjcf', incoming, w_up, preferred_element_type=jnp.f...  10.5 us
    dot_general x1, matrix products, body(): jnp.einsum('pjcd,jfd->pjcf', incoming, w_gate, preferred_element_type=jnp...  9.77 us
    all_gather x1, waiting for transfers between devices, body(): incoming = lax.all_gather(arrived, 'sub', axis=3, tiled=True)  8.87 us
  transfers between devices with their start and end apart: 5, of which 5 were waited for; matrix products, arithmetic and copies ran while one was open for 1% of the time, Pallas kernels for 0%

commit v1 on v0

--- a/solution.py
+++ b/solution.py
@@ -56,7 +56,7 @@
     )
     head_rows = lax.all_to_all(attention, ("tp", "sub"), split_axis=1, concat_axis=0, tiled=True)
     partial_value = jnp.dot(head_rows, out_weight, preferred_element_type=jnp.float32)
-    summed = lax.psum(partial_value, ("tp", "sub"))
+    summed = lax.psum(lax.psum(partial_value, "sub"), "tp")
     attended_all = summed.astype(jnp.bfloat16)
     attended = lax.dynamic_slice_in_dim(attended_all, shard_index * row_count, row_count, 0)
     pool_rows = attended_all.shape[0]

time: 256 us -> 272 us (1.062)
  waiting for transfers between devices: 133 us -> 152 us
  blocking collectives: 40 us -> 36.8 us
    psum x0 -> x1, waiting for transfers between devices: none -> 18.8 us  [body(): summed = lax.psum(lax.psum(partial_value, 'sub'), 'tp')]
  transfers between devices with their start and end apart: 5 -> 6, of which waited for: 5 -> 6; matrix products, arithmetic and copies ran while one was open for 1% -> 1% of each run, Pallas kernels for 0% -> 0%
where the time goes in v1:
time: 272 us; the launch traced here: 271 us
  waiting for transfers between devices  152 us (56%)
  matrix products  36.8 us (14%)
  blocking collectives  36.8 us (14%)
  local copies, waits for them, and re-layouts  17.3 us (6%)
  between operations  13.9 us (5%)
  starting transfers between devices  9.33 us (3%)
  other arithmetic  4.91 us (2%)
    psum x1, waiting for transfers between devices, body(): gate_value, up_value = lax.psum((gate_part, up_part), 'tp')  87 us
    all_to_all x1, blocking collectives, body(): lax.all_to_all(own_slice, 'pool', split_axis=0, concat_axis=0, tiled=True)  26.1 us
    all_to_all x1, waiting for transfers between devices, body(): lax.all_to_all(expert_rows, 'pool', split_axis=0, concat_axis=0, tiled=True)  22.6 us
    psum x1, waiting for transfers between devices, body(): summed = lax.psum(lax.psum(partial_value, 'sub'), 'tp')  18.8 us
    reduce_scatter x1, waiting for transfers between devices, body(): lax.psum_scatter(partial_rows, 'sub', scatter_dimension=3, tiled=True)  11.7 us
    psum x1, blocking collectives, body(): summed = lax.psum(lax.psum(partial_value, 'sub'), 'tp')  10.7 us
    dot_general x1, matrix products, body(): jnp.einsum('pjcd,jfd->pjcf', incoming, w_up, preferred_element_type=jnp.f...  10.5 us
    dot_general x1, matrix products, body(): jnp.einsum('pjcd,jfd->pjcf', incoming, w_gate, preferred_element_type=jnp...  9.77 us
  transfers between devices with their start and end apart: 6, of which 6 were waited for; matrix products, arithmetic and copies ran while one was open for 1% of the time, Pallas kernels for 0%

profile of v1, /device:TPU:0, one launch (start us, length us, event | category | flops | bytes accessed | tf_op | source)
XLA Modules:
  0.0 271.2 jit_solution(18326182148163177034)
XLA Ops:
  7.2 0.0 copy-start
  7.2 0.0 copy-start.3
  7.2 0.0 copy-start.5
  7.2 0.8 copy.48
  8.1 0.7 iota_compare_fusion.8
  8.8 0.0 copy-done
  8.8 0.4 fusion.16
  9.2 0.2 fusion.33
  9.4 1.5 fusion.17
  11.0 0.6 copy.36
  11.6 4.2 %all-to-all-start = ((bf16[4,4,1024]{2,0,1:T(4,128)(2,1)}), bf16[4,4,1024]{2,0,1:T(4,128)(2,1)S(1)}, u32[]{:S(2)}, u32[]{:S(2)}) async-start(bf16[4,4,1024]{2,0,1:T(4,128)(2,1)} %copy.36), calls=%async_computation | async-start | bytes 65536 | tf_op jit(solution)/shard_map/all_to_all | solution.py:57
  15.8 0.0 all-reduce.5.cloned.1.call-start
  15.8 0.0 copy-done.3
  15.8 0.1 copy.37
  15.9 0.1 eq.26
  16.0 0.0 copy-done.5
  16.0 0.2 select_reduce_fusion.1
  16.1 0.1 fusion.26
  16.2 0.2 reduce_window_sum.11
  16.4 0.2 select_reduce_fusion
  16.6 3.1 %all-to-all-done = bf16[4,4,1024]{2,0,1:T(4,128)(2,1)S(1)} async-done(((bf16[4,4,1024]{2,0,1:T(4,128)(2,1)}), bf16[4,4,1024]{2,0,1:T(4,128)(2,1)S(1)}, u32[]{:S(2)}, u32[]{:S(2)}) %all-to-all-start) | async-done | bytes 32800 | tf_op jit(solution)/shard_map/all_to_all | solution.py:57
  19.7 3.5 %fusion.34 = f32[16,2048]{1,0:T(8,128)} fusion(bf16[16,1024]{1,0:T(8,128)(2,1)S(1)} %all_to_all.20, bf16[1024,2048]{1,0:T(8,128)(2,1)} %param.15), kind=kOutput, calls=%fused_computation.55 | convolution fusion | flops 67108864 | bytes 4358144 | tf_op jit(solution)/shard_map/dot_general | solution.py:58
  23.3 0.0 all-reduce.5.cloned.1.call-update
  23.3 0.0 all-gather.2.cloned.1.call-start
  23.4 18.8 %all-reduce.5.cloned.1.call-done = f32[16,2048]{1,0:T(8,128)} async-done(((f32[16,2048]{1,0:T(8,128)}), f32[16,2048]{1,0:T(8,128)}) %all-reduce.5.cloned.1.call-update) | async-done | bytes 131088 | tf_op jit(solution)/shard_map/psum | solution.py:59
  42.1 10.7 %all-reduce.8 = bf16[16,2048]{1,0:T(8,128)(2,1)S(1)} all-reduce(f32[16,2048]{1,0:T(8,128)} %all-reduce.5.cloned.1.call-done), channel_id=1, replica_groups=mesh['grp'=2,'pool'=4,'tp'=2,'sub'=2] {'tp'}, use_global_device_ids=true, to_apply=%region_3.4 | all-reduce | flops 32768 | bytes 196608 | tf_op jit(solution)/shard_map/psum | solution.py:59
  52.8 3.2 %convolution_convert_fusion = bf16[896,2048]{1,0:T(8,128)(2,1)} fusion(bf16[16,2048]{1,0:T(8,128)(2,1)S(1)} %all-reduce.8, s32[128]{0:T(128)S(1)} %get-tuple-element.5, s32[128]{0:T(128)S(1)} %and_select_fusion), kind=kOutput, calls=%fused_computation.9 | convolution fusion | flops 64356352 | bytes 3736576 | tf_op jit(solution)/shard_map/dot_general | solution.py:83
  56.0 6.0 %reshape.116 = bf16[4,16,14,2048]{3,2,1,0:T(8,128)(2,1)} reshape(bf16[896,2048]{1,0:T(8,128)(2,1)} %convolution_convert_fusion) | data formatting | bytes 7340032 | tf_op jit(solution)/shard_map/reshape | solution.py:86
  62.0 1.3 constant_dynamic-slice_fusion
  63.3 0.5 copy.38
  63.9 26.1 %all_to_all.26 = bf16[4,16,14,512]{3,1,2,0:T(8,128)(2,1)S(1)} all-to-all(bf16[4,16,14,512]{3,1,2,0:T(8,128)(2,1)S(1)} %copy.38), channel_id=1, replica_groups=mesh['grp'=2,'pool'=4,'tp'=2,'sub'=2] {'pool'}, dimensions={0} | all-to-all | bytes 1835008 | tf_op jit(solution)/shard_map/all_to_all | solution.py:92
  90.0 1.5 copy.39
  91.5 0.0 all-gather.2.cloned.1.call-update
  91.5 0.0 all-reduce.7.cloned.1.call-start
  91.5 8.8 %all-gather.2.cloned.1.call-done = bf16[4,16,14,1024]{3,2,0,1:T(8,128)(2,1)} async-done(((bf16[4,16,14,512]{3,2,0,1:T(8,128)(2,1)}), bf16[4,16,14,1024]{3,2,0,1:T(8,128)(2,1)}) %all-gather.2.cloned.1.call-update) | async-done | bytes 1835024 | tf_op jit(solution)/shard_map/all_gather | solution.py:93
  100.3 0.0 copy-start.2
  100.3 10.5 %fusion.10 = f32[4,16,14,384]{3,2,0,1:T(8,128)} fusion(bf16[4,16,14,1024]{3,2,0,1:T(8,128)(2,1)} %all-gather.2.cloned.1.call-done, bf16[16,384,1024]{2,1,0:T(8,128)(2,1)} %param.20), kind=kOutput, calls=%fused_computation.12 | convolution fusion | flops 704643072 | bytes 15794176 | tf_op jit(solution)/shard_map/pjcd,jfd->pjcf/dot_general | solution.py:95
  110.8 0.0 copy-done.2
  110.9 9.8 %fusion.7 = f32[4,16,14,384]{3,2,0,1:T(8,128)} fusion(bf16[4,16,14,1024]{3,2,0,1:T(8,128)(2,1)S(1)} %copy-done.2, bf16[16,384,1024]{2,1,0:T(8,128)(2,1)} %param.19), kind=kOutput, calls=%fused_computation.11 | convolution fusion | flops 704643072 | bytes 15794176 | tf_op jit(solution)/shard_map/pjcd,jfd->pjcf/dot_general | solution.py:94
  120.6 0.0 all-reduce.7.cloned.1.call-update
  120.6 0.2 reduce-scatter.2.cloned.1.call-start
  120.9 87.0 %all-reduce.7.cloned.1.call-done = (f32[4,16,14,384]{3,2,0,1:T(8,128)}, f32[4,16,14,384]{3,2,0,1:T(8,128)}) async-done(((f32[4,16,14,384]{3,2,0,1:T(8,128)}, f32[4,16,14,384]{3,2,0,1:T(8,128)}), (f32[4,16,14,384]{3,2,0,1:T(8,128)}, f32[4,16,14,384]{3,2,0,1:T(8,128)})) %all-reduce.7.cloned.1.call-update) | async-done | bytes 2752528 | tf_op jit(solution)/shard_map/psum | solution.py:96
  207.9 7.9 %fusion.1 = f32[16,4,14,1024]{3,2,1,0:T(8,128)S(1)} fusion(bf16[16,384,1024]{2,1,0:T(8,128)(2,1)} %param.21, f32[4,16,14,384]{3,2,0,1:T(8,128)} %get-tuple-element.2, f32[4,16,14,384]{3,2,0,1:T(8,128)} %get-tuple-element.3), kind=kOutput, calls=%fused_computation.2 | convolution fusion | flops 706707456 | bytes 19005440 | tf_op jit(solution)/shard_map/pjcf,jfd->pjcd/dot_general | solution.py:98
  215.8 3.9 %copy.58 = f32[16,4,14,1024]{3,0,2,1:T(8,128)} copy(f32[16,4,14,1024]{3,2,1,0:T(8,128)S(1)} %fusion.1) | data formatting | bytes 7340032 | tf_op jit(solution)/shard_map/pjcf,jfd->pjcd/dot_general | solution.py:98
  219.7 0.0 reduce-scatter.2.cloned.1.call-update
  219.8 0.0 copy-start.4
  219.8 11.7 %reduce-scatter.2.cloned.1.call-done = f32[4,16,14,512]{3,1,2,0:T(8,128)} async-done(((f32[4,16,14,1024]{3,1,2,0:T(8,128)}), f32[4,16,14,512]{3,1,2,0:T(8,128)}) %reduce-scatter.2.cloned.1.call-update) | async-done | bytes 1835024 | tf_op jit(solution)/shard_map/reduce_scatter | solution.py:99
  231.5 2.6 convert_element_type.45
  234.1 4.8 %all-to-all-start.2 = ((bf16[4,16,14,512]{3,1,2,0:T(8,128)(2,1)}), bf16[4,16,14,512]{3,1,2,0:T(8,128)(2,1)S(1)}, u32[]{:S(2)}, u32[]{:S(2)}) async-start(bf16[4,16,14,512]{3,1,2,0:T(8,128)(2,1)} %convert_element_type.45), calls=%async_computation.3 | async-start | bytes 1835008 | tf_op jit(solution)/shard_map/all_to_all | solution.py:102
  238.9 0.1 add.78
  239.0 0.0 copy-done.4
  239.0 0.1 copy.42
  239.1 0.6 constant_dynamic-slice_fusion.1
  239.7 22.6 %all-to-all-done.2 = bf16[4,16,14,512]{3,1,2,0:T(8,128)(2,1)S(1)} async-done(((bf16[4,16,14,512]{3,1,2,0:T(8,128)(2,1)}), bf16[4,16,14,512]{3,1,2,0:T(8,128)(2,1)S(1)}, u32[]{:S(2)}, u32[]{:S(2)}) %all-to-all-start.2) | async-done | bytes 917536 | tf_op jit(solution)/shard_map/all_to_all | solution.py:102
  262.3 0.0 copy-start.1
  262.3 0.5 copy.41
  262.8 0.3 reshape.117
  263.1 0.8 gather_fusion
  263.9 0.8 multiply_reduce_fusion
  264.7 0.0 copy-done.1
  (6 shorter events, 0.1 us)
Async XLA Ops:
  7.2 1.6 copy-start
  7.2 8.6 %copy-start.3 = (s32[16,8]{0,1:T(8,128)S(1)}, s32[16,8]{0,1:T(8,128)}, u32[]{:S(2)}) copy-start(s32[16,8]{0,1:T(8,128)} %param.16) | copy-start | bytes 1540
  7.2 8.8 %copy-start.5 = (s32[64]{0:T(128)S(1)}, s32[64]{0:T(128)}, u32[]{:S(2)}) copy-start(s32[64]{0:T(128)} %param.18) | copy-start | bytes 772
  11.6 8.2 %all-to-all-start = ((bf16[4,4,1024]{2,0,1:T(4,128)(2,1)}), bf16[4,4,1024]{2,0,1:T(4,128)(2,1)S(1)}, u32[]{:S(2)}, u32[]{:S(2)}) async-start(bf16[4,4,1024]{2,0,1:T(4,128)(2,1)} %copy.36), calls=%async_computation | async-start | bytes 65536 | tf_op jit(solution)/shard_map/all_to_all | solution.py:57
  15.8 26.4 %all-reduce.5.cloned.1.call-start = ((), (), s32[]{:S(2)}) async-start(), calls=%async_computation.4 | async-start | bytes 262144 | tf_op jit(solution)/shard_map/psum | solution.py:59
  23.3 77.1 %all-gather.2.cloned.1.call-start = ((), (), s32[]{:S(2)}) async-start(), calls=%async_computation.5 | async-start | bytes 3145728 | tf_op jit(solution)/shard_map/all_gather | solution.py:93
  91.5 116.4 %all-reduce.7.cloned.1.call-start = ((), (), s32[]{:S(2)}) async-start(), calls=%async_computation.7 | async-start | bytes 6291456 | tf_op jit(solution)/shard_map/psum | solution.py:96
  100.3 10.5 %copy-start.2 = (bf16[4,16,14,1024]{3,2,0,1:T(8,128)(2,1)S(1)}, bf16[4,16,14,1024]{3,2,0,1:T(8,128)(2,1)}, u32[]{:S(2)}) copy-start(bf16[4,16,14,1024]{3,2,0,1:T(8,128)(2,1)} %all-gather.2.cloned.1.call-done) | copy-start | bytes 5505028
  120.6 110.8 %reduce-scatter.2.cloned.1.call-start = ((), (), s32[]{:S(2)}) async-start(), calls=%async_computation.6 | async-start | bytes 5505024 | tf_op jit(solution)/shard_map/reduce_scatter | solution.py:99
  219.8 19.2 %copy-start.4 = (f32[16,8]{0,1:T(8,128)S(1)}, f32[16,8]{0,1:T(8,128)}, u32[]{:S(2)}) copy-start(f32[16,8]{0,1:T(8,128)} %param.17) | copy-start | bytes 1540
  234.1 28.2 %all-to-all-start.2 = ((bf16[4,16,14,512]{3,1,2,0:T(8,128)(2,1)}), bf16[4,16,14,512]{3,1,2,0:T(8,128)(2,1)S(1)}, u32[]{:S(2)}, u32[]{:S(2)}) async-start(bf16[4,16,14,512]{3,1,2,0:T(8,128)(2,1)} %convert_element_type.45), calls=%async_computation.3 | async-start | bytes 1835008 | tf_op jit(solution)/shard_map/all_to_all | solution.py:102
  262.3 2.4 copy-start.1
Sparse Core Ops, SparseCore 0:
  23.4 18.6 all-reduce.4
  91.6 8.6 all-gather.1
  120.8 87.1 all-reduce.6
  219.9 11.5 reduce-scatter.1
